TPU v7x, 32 devices: a whole 2x2x4 slice. The times are simulated.
32 devices in a mesh: grp: 2 (over y), row: 4 (over z), col: 4 (over x, core).
Axes of the slice: x: 2, y: 2, z: 4, core: 2. Of those that a mesh axis runs over, the one named last changes fastest.
Arguments:
- activations: bfloat16 [1024, 6144], P(('grp', 'col'), 'row'), parts along dimension 0, may hold values from -6 to 6
- out_grads: bfloat16 [1024, 18432], P(('grp', 'row'), 'col'), parts along dimension 0, may hold values from -0.1796875 to 0.1796875
- matrix: bfloat16 [12288, 18432], P(('grp', 'row'), 'col'), parts along dimension 0, may hold values from -30 to 30
- left: bfloat16 [12288, 256], P(('grp', 'row')), parts along dimension 0, may hold values from -4 to 4
- right: bfloat16 [36864, 256], P(('grp', 'col')), parts along dimension 0, may hold values from -4 to 4
Outputs:
- left_new: bfloat16 [12288, 256], P(('grp', 'row')), parts along dimension 0
- right_new: bfloat16 [36864, 256], P(('grp', 'col')), parts along dimension 0
- residual: bfloat16 [12288, 18432], P(('grp', 'row'), 'col'), parts along dimension 0
There are 2 independent parts, one for each index of `grp`. A program takes and returns all parts, laid end to end along the dimension named above; each array names one. Nothing has to cross between parts.
All inputs are finite; a program needn't handle non-finite values.
Results may differ from a plain program's by a relative error of at most 0.0034.
Values may be sent and summed in bfloat16 or wider, within the bound.
A program may use at most 192 MiB of HBM per device.

v0:
```python
import jax
import jax.numpy as jnp
from jax import lax
from jax.sharding import PartitionSpec as P

epsilon = 1e-06


def contract_rank(first, second):
    return lax.dot_general(
        first, second, (((1,), (1,)), ((), ())), preferred_element_type=jnp.float32
    )


def contract_tokens(first, second):
    return lax.dot_general(
        first, second, (((0,), (0,)), ((), ())), preferred_element_type=jnp.float32
    )


def body(activations, out_grads, matrix, left, right):
    col_count = lax.axis_size("col")
    row_count = lax.axis_size("row")
    gathered = lax.all_gather(activations, "col", axis=0, tiled=True)
    grads_full = lax.all_gather(out_grads, "row", axis=0, tiled=True)
    gradient = contract_tokens(gathered, grads_full)
    wfloat = matrix.astype(jnp.float32)
    fisher = 1.0 + (wfloat * gradient) ** 2
    early_residual = wfloat - contract_rank(left, right)
    weighted_early = (fisher * early_residual).astype(jnp.bfloat16)
    left_partial = jnp.dot(weighted_early, right, preferred_element_type=jnp.float32)
    left_descent = lax.psum(left_partial, "col")
    left_round = left_descent.astype(jnp.bfloat16)
    left_norm_term = jnp.sum(left_descent * left_descent) / col_count
    left_image = contract_rank(left_round, right)
    left_curve, left_norm = lax.psum(
        (jnp.sum(fisher * left_image * left_image), left_norm_term), ("row", "col")
    )
    left_step = left_norm / (left_curve + epsilon)
    left_new = (left.astype(jnp.float32) + left_step * left_descent).astype(jnp.bfloat16)
    later_residual = early_residual - left_step * left_image
    weighted_later = (fisher * later_residual).astype(jnp.bfloat16)
    right_partial = contract_tokens(weighted_later, left_new)
    right_descent = lax.psum(right_partial.astype(jnp.bfloat16), "row").astype(jnp.float32)
    right_round = right_descent.astype(jnp.bfloat16)
    right_norm_term = jnp.sum(right_descent * right_descent) / row_count
    right_image = contract_rank(left_new, right_round)
    right_curve, right_norm = lax.psum(
        (jnp.sum(fisher * right_image * right_image), right_norm_term), ("row", "col")
    )
    right_step = right_norm / (right_curve + epsilon)
    right_new = (right.astype(jnp.float32) + right_step * right_descent).astype(jnp.bfloat16)
    residual = (later_residual - right_step * right_image).astype(jnp.bfloat16)
    return (left_new, right_new, residual)


def solution(mesh):
    placed = (
        P(("grp", "col"), "row"),
        P(("grp", "row"), "col"),
        P(("grp", "row"), "col"),
        P(("grp", "row"), None),
        P(("grp", "col"), None),
    )
    return jax.shard_map(
        body,
        mesh=mesh,
        in_specs=placed,
        out_specs=(P(("grp", "row"), None), P(("grp", "col"), None), P(("grp", "row"), "col")),
        check_vma=False,
    )
```

profile of v0, /device:TPU:0, one launch (start us, length us, event | category | flops | bytes accessed | tf_op | source)
XLA Modules:
  0.0 489.8 jit_solution(9094421947014775079)
XLA Ops:
  7.2 0.0 all-gather.3.cloned.1.call-start
  7.2 0.7 all-gather.3.cloned.1.call-update
  7.9 0.0 all-gather.5.cloned.1.call-start
  7.9 0.7 all-gather.5.cloned.1.call-update
  8.6 0.0 all-reduce.5.cloned.1.call-start
  8.7 19.6 %convert_subtract_fusion = f32[1536,4608]{1,0:T(8,128)} fusion(bf16[1536,4608]{1,0:T(8,128)(2,1)} %param.7, bf16[1536,256]{1,0:T(8,128)(2,1)} %param.8, bf16[4608,256]{1,0:T(8,128)(2,1)} %param.9), kind=kOutput, calls=%fused_computation.2 | convolution fusion | flops 3638034432 | bytes 45613056 | tf_op jit(solution)/shard_map/dot_general | solution.py:10
  28.3 0.0 copy-start
  28.3 3.6 all-gather.3.cloned.1.call-done
  31.9 91.0 %all-gather.5.cloned.1.call-done = bf16[512,4608]{1,0:T(8,128)(2,1)} async-done(((bf16[128,4608]{1,0:T(8,128)(2,1)}), bf16[512,4608]{1,0:T(8,128)(2,1)}) %all-gather.5.cloned.1.call-update) | async-done | bytes 4718608 | tf_op jit(solution)/shard_map/all_gather | solution.py:25
  122.9 17.9 %fusion.1 = f32[1536,4608]{1,0:T(8,128)} fusion(bf16[1536,4608]{1,0:T(8,128)(2,1)} %param.7, bf16[512,1536]{1,0:T(8,128)(2,1)} %all-gather.3.cloned.1.call-done, bf16[512,4608]{1,0:T(8,128)(2,1)} %all-gather.5.cloned.1.call-done), kind=kOutput, calls=%fused_computation.5 | convolution fusion | flops 7276068864 | bytes 48758784 | tf_op jit(solution)/shard_map/dot_general | solution.py:16
  140.8 0.0 copy-done
  140.8 19.9 %fusion.4 = f32[1536,256]{1,0:T(8,128)} fusion(bf16[4608,256]{1,0:T(8,128)(2,1)S(1)} %copy-done, f32[1536,4608]{1,0:T(8,128)} %fusion.1, f32[1536,4608]{1,0:T(8,128)} %convert_subtract_fusion), kind=kOutput, calls=%fused_computation.12 | convolution fusion | flops 3638034432 | bytes 60555264 | tf_op jit(solution)/shard_map/dot_general | solution.py:31
  160.7 0.0 all-reduce.5.cloned.1.call-update
  160.7 0.2 all-reduce.7.cloned.1.call-start
  160.9 41.2 %all-reduce.5.cloned.1.call-done = f32[1536,256]{1,0:T(8,128)} async-done(((f32[1536,256]{1,0:T(8,128)}), f32[1536,256]{1,0:T(8,128)}) %all-reduce.5.cloned.1.call-update) | async-done | bytes 1572880 | tf_op jit(solution)/shard_map/psum | solution.py:32
  202.1 2.4 multiply_reduce_fusion
  205.2 23.8 %fusion.2 = (f32[]{:T(128)}, f32[1536,4608]{1,0:T(8,128)}) fusion(f32[1536,4608]{1,0:T(8,128)} %fusion.1, bf16[4608,256]{1,0:T(8,128)(2,1)S(1)} %copy-done, f32[1536,256]{1,0:T(8,128)} %all-reduce.5.cloned.1.call-done), kind=kOutput, calls=%fused_computation.6 | convolution fusion | flops 3645505536 | bytes 60555268 | tf_op jit(solution)/shard_map/dot_general | solution.py:10
  229.0 32.8 %all-reduce.1 = (f32[]{:T(128)}, f32[]{:T(128)}) all-reduce(f32[]{:T(128)S(6)} %div.12, f32[]{:T(128)} %get-tuple-element.7), channel_id=1, replica_groups=mesh['grp'=2,'row'=4,'col'=4] {'row','col'}, use_global_device_ids=true, to_apply=%region_2.0 | all-reduce | flops 2 | bytes 16 | tf_op jit(solution)/shard_map/psum | solution.py:36
  263.1 1.8 add_convert_fusion
  264.9 0.0 copy-start.2
  264.9 30.2 %fusion.6 = bf16[4608,256]{1,0:T(8,128)(2,1)} fusion(bf16[1536,256]{1,0:T(8,128)(2,1)S(1)} %add_convert_fusion, f32[1536,4608]{1,0:T(8,128)} %fusion.1, f32[1536,4608]{1,0:T(8,128)} %convert_subtract_fusion, f32[1536,4608]{1,0:T(8,128)} %get-tuple-element.8, f32[]{:T(128)S(6)} %div.13), kind=kOutput, calls=%fused_computation.14 | convolution fusion | flops 3653369856 | bytes 88080384 | tf_op jit(solution)/shard_map/dot_general | solution.py:16
  295.1 0.0 all-reduce.7.cloned.1.call-update
  295.2 92.0 %all-reduce.7.cloned.1.call-done = bf16[4608,256]{1,0:T(8,128)(2,1)} async-done(((bf16[4608,256]{1,0:T(8,128)(2,1)}), bf16[4608,256]{1,0:T(8,128)(2,1)}) %all-reduce.7.cloned.1.call-update) | async-done | bytes 2359312 | tf_op jit(solution)/shard_map/psum | solution.py:44
  387.2 3.5 fusion.7
  391.3 0.0 copy-done.2
  391.3 23.9 %fusion.3 = (f32[]{:T(128)}, f32[1536,4608]{1,0:T(8,128)}) fusion(f32[1536,4608]{1,0:T(8,128)} %fusion.1, bf16[1536,256]{1,0:T(8,128)(2,1)S(1)} %add_convert_fusion, bf16[4608,256]{1,0:T(8,128)(2,1)} %all-reduce.7.cloned.1.call-done), kind=kOutput, calls=%fused_computation.7 | convolution fusion | flops 3645112320 | bytes 59768836 | tf_op jit(solution)/shard_map/dot_general | solution.py:10
  415.2 32.0 %all-reduce = (f32[]{:T(128)}, f32[]{:T(128)}) all-reduce(f32[]{:T(128)S(6)} %div.14, f32[]{:T(128)} %get-tuple-element.9), channel_id=1, replica_groups=mesh['grp'=2,'row'=4,'col'=4] {'row','col'}, use_global_device_ids=true, to_apply=%region_7.0 | all-reduce | flops 2 | bytes 16 | tf_op jit(solution)/shard_map/psum | solution.py:48
  448.5 0.0 copy-start.1
  448.5 32.5 %subtract_convert_fusion = bf16[1536,4608]{1,0:T(8,128)(2,1)} fusion(f32[1536,4608]{1,0:T(8,128)} %get-tuple-element.10, f32[]{:T(128)S(6)} %div.15, f32[1536,4608]{1,0:T(8,128)} %convert_subtract_fusion, f32[1536,4608]{1,0:T(8,128)} %get-tuple-element.8, f32[]{:T(128)S(6)} %div.13), kind=kLoop, calls=%fused_computation.8 | loop fusion | flops 35389440 | bytes 99090440 | tf_op jit(solution)/shard_map/convert_element_type | solution.py:53
  481.0 0.0 copy-done.1
  481.0 2.3 fusion.9
Async XLA Ops:
  7.2 24.8 %all-gather.3.cloned.1.call-start = ((), (), s32[]{:S(2)}) async-start(), calls=%async_computation | async-start | bytes 1966080 | tf_op jit(solution)/shard_map/all_gather | solution.py:24
  7.9 115.0 %all-gather.5.cloned.1.call-start = ((), (), s32[]{:S(2)}) async-start(), calls=%async_computation.1 | async-start | bytes 5898240 | tf_op jit(solution)/shard_map/all_gather | solution.py:25
  8.6 193.4 %all-reduce.5.cloned.1.call-start = ((), (), s32[]{:S(2)}) async-start(), calls=%async_computation.2 | async-start | bytes 3145728 | tf_op jit(solution)/shard_map/psum | solution.py:32
  28.3 112.5 %copy-start = (bf16[4608,256]{1,0:T(8,128)(2,1)S(1)}, bf16[4608,256]{1,0:T(8,128)(2,1)}, u32[]{:S(2)}) copy-start(bf16[4608,256]{1,0:T(8,128)(2,1)} %param.9) | copy-start | bytes 7077892
  160.7 226.5 %all-reduce.7.cloned.1.call-start = ((), (), s32[]{:S(2)}) async-start(), calls=%async_computation.3 | async-start | bytes 4718592 | tf_op jit(solution)/shard_map/psum | solution.py:44
  264.9 126.4 %copy-start.2 = (bf16[1536,256]{1,0:T(8,128)(2,1)}, bf16[1536,256]{1,0:T(8,128)(2,1)S(1)}, u32[]{:S(2)}) copy-start(bf16[1536,256]{1,0:T(8,128)(2,1)S(1)} %add_convert_fusion) | copy-start | bytes 2359300
  448.5 32.6 %copy-start.1 = (bf16[4608,256]{1,0:T(8,128)(2,1)S(1)}, bf16[4608,256]{1,0:T(8,128)(2,1)}, u32[]{:S(2)}) copy-start(bf16[4608,256]{1,0:T(8,128)(2,1)} %all-reduce.7.cloned.1.call-done) | copy-start | bytes 7077892
Sparse Core Ops, SparseCore 0:
  9.5 22.3 all-gather.2
  33.5 89.3 all-gather.4
  160.8 41.2 all-reduce.4
  295.3 91.8 all-reduce.6
where the time goes:
time: 490 us
  waiting for transfers between devices  229 us (47%)
  matrix products  135 us (28%)
  blocking collectives  64.8 us (13%)
  other arithmetic  42.5 us (9%)
  between operations  17.7 us (4%)
    psum x1, waiting for transfers between devices, body(): lax.psum(right_partial.astype(jnp.bfloat16), 'row').astype(jnp.float32)  92 us
    all_gather x1, waiting for transfers between devices, body(): grads_full = lax.all_gather(out_grads, 'row', axis=0, tiled=True)  91 us
    dot_general x3, matrix products, contract_rank(): lax.dot_general(first, second, (((1,), (1,)), ((), ())), preferred_elemen...  67.3 us
    dot_general x2, matrix products, contract_tokens(): lax.dot_general(first, second, (((0,), (0,)), ((), ())), preferred_elemen...  48.1 us
    psum x1, waiting for transfers between devices, body(): left_descent = lax.psum(left_partial, 'col')  41.2 us
    psum x1, blocking collectives, body(): lax.psum((jnp.sum(fisher * left_image * left_image), left_norm_term), ('r...  32.8 us
    convert_element_type x1, other arithmetic, body(): residual = (later_residual - right_step * right_image).astype(jnp.bfloat16)  32.5 us
    psum x1, blocking collectives, body(): lax.psum((jnp.sum(fisher * right_image * right_image), right_norm_term),...  32 us
  transfers between devices with their start and end apart: 4, of which 4 were waited for; matrix products, arithmetic and copies ran while one was open for 4% of the time, Pallas kernels for 0%

commit v1 on v0

v1 whole, which is shorter than its diff:
```python
import functools

import jax
import jax.numpy as jnp
from jax import lax
from jax.experimental import pallas as pl
from jax.experimental.pallas import tpu as pltpu
from jax.sharding import PartitionSpec as P

epsilon = 1e-06
f32 = jnp.float32
bf16 = jnp.bfloat16
MESH = pl.DeviceIdType.MESH


def pick(extent, cap, unit):
    best = unit
    for size in range(unit, cap + 1, unit):
        if extent % size == 0:
            best = size
    return best


def mm(a, b):
    return jnp.dot(a, b, preferred_element_type=f32)


def mm_nt(a, b):
    return lax.dot_general(a, b, (((1,), (1,)), ((), ())), preferred_element_type=f32)


def main_kernel(
    nr, nc, nch, chunk, tile,
    act_hbm, og_hbm, w_hbm, l_ref, r_ref,
    ln_ref, ldr_ref, t_hbm, s_ref,
    fisher, wbuf, ogb, actb, actt, lpart, lsend, lr1, lh, lr2, ld4, lnt,
    part, inb, exb, tot, rp, acc, sc, sr,
    wsem, ogsem, asem, act_s, act_r, up_s, up_r, dn_s, dn_r,
    l1, l2s, l2r, l3s, l3r, l4, cs, cr, rs, rr,
    in_s, in_r, ex_s, ex_r, out_s, out_r, tsem,
):
    g = lax.axis_index("grp")
    r = lax.axis_index("row")
    c = lax.axis_index("col")
    nx = nc // 2
    rows = l_ref.shape[0]
    q = rows // nc
    nt = rows // tile
    lanes = pick(rows, 256, 128)

    def at(row, col):
        return (g, row, col)

    def remote(src, dst, ss, rs_, dev):
        return pltpu.make_async_remote_copy(
            src_ref=src, dst_ref=dst, send_sem=ss, recv_sem=rs_, device_id=dev, device_id_type=MESH
        )

    def w_copy(k, slot):
        cols = pl.ds(pl.multiple_of(k * chunk, 128), chunk)
        return pltpu.make_async_copy(w_hbm.at[:, cols], wbuf.at[slot], wsem.at[slot])

    def og_local(k):
        cols = pl.ds(pl.multiple_of(k * chunk, 128), chunk)
        return pltpu.make_async_copy(og_hbm.at[:, cols], ogb.at[k, r], ogsem.at[k])

    act_local = pltpu.make_async_copy(act_hbm, actb.at[c], asem)
    act_local.start()

    def start_og(k, carry):
        og_local(k).start()
        return carry

    lax.fori_loop(0, nch, start_og, 0)
    w_copy(0, 0).start()

    bar = pltpu.get_barrier_semaphore()
    for d in range(1, nr):
        pl.semaphore_signal(bar, inc=1, device_id=at(lax.rem(r + d, nr), c), device_id_type=MESH)
    for d in range(1, nc):
        pl.semaphore_signal(bar, inc=1, device_id=at(r, lax.rem(c + d, nc)), device_id_type=MESH)
    pl.semaphore_wait(bar, nr + nc - 2)

    act_local.wait()

    def act_copy(d):
        return remote(actb.at[c], actb.at[c], act_s.at[d - 1], act_r.at[d - 1], at(r, lax.rem(c + d, nc)))

    for d in range(1, nc):
        act_copy(d).start()

    def up_copy(k, s):
        blk = jnp.maximum(r - s, 0)
        return remote(ogb.at[k, blk], ogb.at[k, blk], up_s.at[k, s], up_r.at[k, s], at(jnp.minimum(r + 1, nr - 1), c))

    def dn_copy(k, s):
        blk = jnp.minimum(r + s, nr - 1)
        return remote(ogb.at[k, blk], ogb.at[k, blk], dn_s.at[k, s], dn_r.at[k, s], at(jnp.maximum(r - 1, 0), c))

    def up_sends(s):
        return jnp.logical_and(r - s >= 0, r + 1 < nr)

    def dn_sends(s):
        return jnp.logical_and(r + s < nr, r >= 1)

    def up_wait(k, s):
        blk = jnp.maximum(r - 1 - s, 0)
        remote(ogb.at[k, blk], ogb.at[k, blk], up_s.at[k, s], up_r.at[k, s], at(jnp.minimum(r + 1, nr - 1), c)).wait_recv()

    def dn_wait(k, s):
        blk = jnp.minimum(r + 1 + s, nr - 1)
        remote(ogb.at[k, blk], ogb.at[k, blk], dn_s.at[k, s], dn_r.at[k, s], at(jnp.maximum(r - 1, 0), c)).wait_recv()

    lpart[...] = jnp.zeros_like(lpart)
    acc[...] = jnp.zeros_like(acc)

    def rows_at(i):
        return pl.ds(pl.multiple_of(i * tile, tile), tile)

    def cols_at(k):
        return pl.ds(pl.multiple_of(k * chunk, chunk), chunk)

    def pass_a(k):
        slot = lax.rem(k, 2)
        w_copy(lax.rem(k + 1, nch), lax.rem(k + 1, 2)).start()
        w_copy(k, slot).wait()

        def step(i, carry):
            rw = rows_at(i)
            og = ogb[k].reshape(-1, chunk)
            grad = mm(actt[rw, :], og)
            w = wbuf[slot, rw, :].astype(f32)
            rj = r_ref[cols_at(k), :]
            wg = w * grad
            fish = 1.0 + wg * wg
            fisher[k, rw, :] = fish
            early = w - mm_nt(l_ref[rw, :], rj)
            lpart[rw, :] += mm((fish * early).astype(bf16), rj)
            return carry

        lax.fori_loop(0, nt, step, 0)

    def gather_step(j, carry):
        @pl.when(j < nch)
        def _():
            og_local(j).wait()

            @pl.when(up_sends(0))
            def _():
                up_copy(j, 0).start()

            @pl.when(dn_sends(0))
            def _():
                dn_copy(j, 0).start()

        for s in range(1, nr):
            k = j - s

            @pl.when(jnp.logical_and(k >= 0, k < nch))
            def _():
                @pl.when(r - s >= 0)
                def _():
                    up_wait(k, s - 1)

                @pl.when(up_sends(s))
                def _():
                    up_copy(k, s).start()

                @pl.when(r + s < nr)
                def _():
                    dn_wait(k, s - 1)

                @pl.when(dn_sends(s))
                def _():
                    dn_copy(k, s).start()

        @pl.when(j == nr - 1)
        def _():
            for d in range(1, nc):
                src = lax.rem(c + nc - d, nc)
                remote(actb.at[src], actb.at[src], act_s.at[d - 1], act_r.at[d - 1], at(r, src)).wait_recv()

            def turn(i, carry):
                rw = pl.ds(pl.multiple_of(i * lanes, lanes), lanes)
                block = actb[:, :, rw].reshape(-1, lanes)
                actt[rw, :] = block.astype(f32).T.astype(bf16)
                return carry

            lax.fori_loop(0, rows // lanes, turn, 0)

        @pl.when(j >= nr - 1)
        def _():
            pass_a(j - (nr - 1))

        return carry

    lax.fori_loop(0, nch + nr - 1, gather_step, 0)

    def drain_og(k, carry):
        for s in range(nr - 1):
            @pl.when(up_sends(s))
            def _():
                up_copy(k, s).wait_send()

            @pl.when(dn_sends(s))
            def _():
                dn_copy(k, s).wait_send()
        return carry

    par = lax.rem(c, 2)
    x = c // 2
    mate = at(r, c + 1 - 2 * par)
    for k in range(nc):
        lsend[k % 2, k // 2] = lpart[k * q:(k + 1) * q, :].astype(bf16)
    one = remote(lsend.at[1 - par], lr1, l1.at[0], l1.at[1], mate)
    one.start()
    one.wait()

    def own_rows(xx):
        return lpart[pl.ds(pl.multiple_of((2 * xx + par) * q, 8), q), :] + lr1[xx].astype(f32)

    for d in range(1, nx):
        xx = lax.rem(x + d, nx)
        lh[d - 1] = own_rows(xx).astype(bf16)
        remote(lh.at[d - 1], lr2.at[d - 1], l2s.at[d - 1], l2r.at[d - 1], at(r, 2 * xx + par)).start()
    desc = own_rows(x)
    for d in range(1, nx):
        xx = lax.rem(x + d, nx)
        remote(lh.at[d - 1], lr2.at[d - 1], l2s.at[d - 1], l2r.at[d - 1], at(r, 2 * xx + par)).wait()
        desc = desc + lr2[d - 1].astype(f32)
    norm = jnp.sum(jnp.sum(desc * desc, axis=0, keepdims=True), axis=1, keepdims=True)
    ld4[par, x] = desc.astype(bf16)
    for d in range(1, nx):
        xx = lax.rem(x + d, nx)
        remote(ld4.at[par, x], ld4.at[par, x], l3s.at[d - 1], l3r.at[d - 1], at(r, 2 * xx + par)).start()
    for d in range(1, nx):
        xx = lax.rem(x + nx - d, nx)
        got = remote(ld4.at[par, xx], ld4.at[par, xx], l3s.at[d - 1], l3r.at[d - 1], at(r, 2 * xx + par))
        got.wait_recv()
    remote(ld4.at[par], ld4.at[par], l4.at[0], l4.at[1], mate).start()
    remote(ld4.at[1 - par], ld4.at[1 - par], l4.at[0], l4.at[1], mate).wait_recv()
    for k in range(nc):
        lpart[k * q:(k + 1) * q, :] = ld4[k % 2, k // 2].astype(f32)

    def cast_left(i, carry):
        ldr_ref[rows_at(i), :] = lpart[rows_at(i), :].astype(bf16)
        return carry

    lax.fori_loop(0, nt, cast_left, 0)

    def curve_tile(fish, image):
        weighted = fish * image * image
        acc[...] += jnp.sum(weighted.reshape(tile // 8, 8, chunk), axis=0)

    def pass_b(k, carry):
        def step(i, inner):
            rw = rows_at(i)
            curve_tile(fisher[k, rw, :], mm_nt(ldr_ref[rw, :], r_ref[cols_at(k), :]))
            return inner

        return lax.fori_loop(0, nt, step, carry)

    lax.fori_loop(0, nch, pass_b, 0)

    def total(t, norm_part):
        curve = jnp.sum(jnp.sum(acc[...], axis=0, keepdims=True), axis=1, keepdims=True)
        top = lax.broadcasted_iota(jnp.int32, (8, 128), 0) == 0
        sc[t, c] = jnp.where(top, jnp.broadcast_to(curve, (8, 128)), jnp.broadcast_to(norm_part, (8, 128)))
        for d in range(1, nc):
            remote(sc.at[t, c], sc.at[t, c], cs.at[t, d - 1], cr.at[t, d - 1], at(r, lax.rem(c + d, nc))).start()
        for d in range(1, nc):
            src = lax.rem(c + nc - d, nc)
            remote(sc.at[t, src], sc.at[t, src], cs.at[t, d - 1], cr.at[t, d - 1], at(r, src)).wait_recv()
        sr[t, r] = jnp.sum(sc[t], axis=0)
        for d in range(1, nr):
            remote(sr.at[t, r], sr.at[t, r], rs.at[t, d - 1], rr.at[t, d - 1], at(lax.rem(r + d, nr), c)).start()
        for d in range(1, nr):
            src = lax.rem(r + nr - d, nr)
            remote(sr.at[t, src], sr.at[t, src], rs.at[t, d - 1], rr.at[t, d - 1], at(src, c)).wait_recv()
        both = jnp.sum(sr[t], axis=0)
        return both[1:2, :] / (both[0:1, :] + epsilon)

    s_ref[0:1, :] = total(0, norm)

    def make_left(i, carry):
        rw = rows_at(i)
        new = (l_ref[rw, :].astype(f32) + s_ref[0:1, 0:1] * lpart[rw, :]).astype(bf16)
        ln_ref[rw, :] = new
        lnt[i] = new.astype(f32).T.astype(bf16)
        return carry

    lax.fori_loop(0, nt, make_left, 0)
    acc[...] = jnp.zeros_like(acc)

    half = nr // 2
    lower = r < half
    inn = at(jnp.where(lower, r + 1, r - 1), c)
    outn = at(jnp.where(lower, jnp.maximum(r - 1, 0), jnp.minimum(r + 1, nr - 1)), c)
    mid = jnp.logical_or(r == half - 1, r == half)
    edge = jnp.logical_or(r == 0, r == nr - 1)
    not_mid = jnp.logical_not(mid)
    not_edge = jnp.logical_not(edge)

    def in_copy(k):
        return remote(part.at[k], inb.at[k], in_s.at[k], in_r.at[k], inn)

    def ex_copy(k):
        return remote(part.at[k], exb.at[k], ex_s.at[k], ex_r.at[k], inn)

    def out_copy(k):
        return remote(tot.at[k], tot.at[k], out_s.at[k], out_r.at[k], outn)

    def pass_c(k):
        slot = lax.rem(k + nch, 2)

        @pl.when(k + 1 < nch)
        def _():
            w_copy(k + 1, lax.rem(k + 1 + nch, 2)).start()

        w_copy(k, slot).wait()
        rp[...] = jnp.zeros_like(rp)

        def step(i, carry):
            rw = rows_at(i)
            rj = r_ref[cols_at(k), :]
            later = wbuf[slot, rw, :].astype(f32) - mm_nt(l_ref[rw, :], rj)
            later = later - s_ref[0:1, 0:1] * mm_nt(ldr_ref[rw, :], rj)
            rp[...] += mm(lnt[i], (fisher[k, rw, :] * later).astype(bf16))
            return carry

        lax.fori_loop(0, nt, step, 0)
        part[k] = rp[...].astype(bf16)

    def pass_d(k):
        def step(i, carry):
            rw = rows_at(i)
            curve_tile(fisher[k, rw, :], mm(ln_ref[rw, :], tot[k]))
            return carry

        lax.fori_loop(0, nt, step, 0)

    lag = 2

    def right_step(j, carry):
        @pl.when(j < nch)
        def _():
            pass_c(j)

            @pl.when(jnp.logical_and(edge, not_mid))
            def _():
                in_copy(j).start()

        a = j - lag

        @pl.when(jnp.logical_and(a >= 0, a < nch))
        def _():
            @pl.when(not_edge)
            def _():
                in_copy(a).wait_recv()
                part[a] = (part[a].astype(f32) + inb[a].astype(f32)).astype(bf16)

            @pl.when(mid)
            def _():
                ex_copy(a).start()

            @pl.when(jnp.logical_and(not_mid, not_edge))
            def _():
                in_copy(a).start()

        b = j - 2 * lag

        @pl.when(jnp.logical_and(b >= 0, b < nch))
        def _():
            @pl.when(mid)
            def _():
                ex_copy(b).wait_recv()
                tot[b] = (part[b].astype(f32) + exb[b].astype(f32)).astype(bf16)

                @pl.when(not_edge)
                def _():
                    out_copy(b).start()

        e = j - 3 * lag

        @pl.when(e >= 0)
        def _():
            @pl.when(not_mid)
            def _():
                out_copy(e).wait_recv()

                @pl.when(not_edge)
                def _():
                    out_copy(e).start()

            pltpu.make_async_copy(tot.at[e], t_hbm.at[e], tsem.at[e]).start()
            pass_d(e)

        return carry

    lax.fori_loop(0, nch + 3 * lag, right_step, 0)

    def square(k, carry):
        t = tot[k].astype(f32)
        return carry + jnp.sum(t * t, axis=0, keepdims=True)

    norm_row = lax.fori_loop(0, nch, square, jnp.zeros((1, chunk), f32))
    s_ref[1:2, :] = total(1, jnp.sum(norm_row, axis=1, keepdims=True) / nr)

    lax.fori_loop(0, nch, drain_og, 0)
    for d in range(1, nc):
        act_copy(d).wait_send()
    for d in range(1, nx):
        remote(ld4.at[par, x], ld4.at[par, x], l3s.at[d - 1], l3r.at[d - 1], mate).wait_send()
    remote(ld4.at[par], ld4.at[par], l4.at[0], l4.at[1], mate).wait_send()
    for t in range(2):
        for d in range(1, nc):
            remote(sc.at[t, c], sc.at[t, c], cs.at[t, d - 1], cr.at[t, d - 1], mate).wait_send()
        for d in range(1, nr):
            remote(sr.at[t, r], sr.at[t, r], rs.at[t, d - 1], rr.at[t, d - 1], inn).wait_send()

    def drain_right(k, carry):
        pltpu.make_async_copy(tot.at[k], t_hbm.at[k], tsem.at[k]).wait()

        @pl.when(not_mid)
        def _():
            in_copy(k).wait_send()

        @pl.when(mid)
        def _():
            ex_copy(k).wait_send()

        @pl.when(not_edge)
        def _():
            out_copy(k).wait_send()
        return carry

    lax.fori_loop(0, nch, drain_right, 0)


def final_kernel(nch, chunk, s_ref, w_ref, l_ref, ldr_ref, ln_ref, r_ref, t_ref, o_ref):
    s1 = s_ref[0:1, 0:1]
    s2 = s_ref[1:2, 0:1]
    for k in range(nch):
        cols = slice(k * chunk, (k + 1) * chunk)
        rj = r_ref[cols, :]
        out = w_ref[:, cols].astype(f32) - mm_nt(l_ref[...], rj) - s1 * mm_nt(ldr_ref[...], rj)
        o_ref[:, cols] = (out - s2 * mm(ln_ref[...], t_ref[k])).astype(bf16)


def body(nr, nc, activations, out_grads, matrix, left, right):
    rows, cols = matrix.shape
    rank = left.shape[1]
    ctok = activations.shape[0]
    rtok = out_grads.shape[0]
    chunk = pick(cols, 512, 128)
    nch = cols // chunk
    tile = pick(rows, 256, 16)
    nx = nc // 2
    q = rows // nc
    dma = pltpu.SemaphoreType.DMA
    any_spec = pl.BlockSpec(memory_space=pl.ANY)
    vmem = pl.BlockSpec(memory_space=pltpu.VMEM)
    px = max(nx - 1, 1)
    pr = max(nr - 1, 1)
    pc = max(nc - 1, 1)
    left_new, left_round, right_t, steps = pl.pallas_call(
        functools.partial(main_kernel, nr, nc, nch, chunk, tile),
        out_shape=(
            jax.ShapeDtypeStruct((rows, rank), bf16),
            jax.ShapeDtypeStruct((rows, rank), bf16),
            jax.ShapeDtypeStruct((nch, rank, chunk), bf16),
            jax.ShapeDtypeStruct((2, 128), f32),
        ),
        in_specs=[any_spec, any_spec, any_spec, vmem, vmem],
        out_specs=(vmem, vmem, any_spec, vmem),
        scratch_shapes=[
            pltpu.VMEM((nch, rows, chunk), f32),
            pltpu.VMEM((2, rows, chunk), bf16),
            pltpu.VMEM((nch, nr, rtok, chunk), bf16),
            pltpu.VMEM((nc, ctok, rows), bf16),
            pltpu.VMEM((rows, nc * ctok), bf16),
            pltpu.VMEM((rows, rank), f32),
            pltpu.VMEM((2, nx, q, rank), bf16),
            pltpu.VMEM((nx, q, rank), bf16),
            pltpu.VMEM((px, q, rank), bf16),
            pltpu.VMEM((px, q, rank), bf16),
            pltpu.VMEM((2, nx, q, rank), bf16),
            pltpu.VMEM((rows // tile, rank, tile), bf16),
            pltpu.VMEM((nch, rank, chunk), bf16),
            pltpu.VMEM((nch, rank, chunk), bf16),
            pltpu.VMEM((nch, rank, chunk), bf16),
            pltpu.VMEM((nch, rank, chunk), bf16),
            pltpu.VMEM((rank, chunk), f32),
            pltpu.VMEM((8, chunk), f32),
            pltpu.VMEM((2, nc, 8, 128), f32),
            pltpu.VMEM((2, nr, 8, 128), f32),
            dma((2,)), dma((nch,)), dma, dma((pc,)), dma((pc,)),
            dma((nch, pr)), dma((nch, pr)), dma((nch, pr)), dma((nch, pr)),
            dma((2,)), dma((px,)), dma((px,)), dma((px,)), dma((px,)), dma((2,)),
            dma((2, pc)), dma((2, pc)), dma((2, pr)), dma((2, pr)),
            dma((nch,)), dma((nch,)), dma((nch,)), dma((nch,)), dma((nch,)), dma((nch,)), dma((nch,)),
        ],
        compiler_params=pltpu.CompilerParams(
            collective_id=0, has_side_effects=True, vmem_limit_bytes=66_500_000
        ),
        name="factor_steps",
    )(activations, out_grads, matrix, left, right)
    ft = pick(rows, 256, 16)
    block = lambda width: pl.BlockSpec((ft, width), lambda i: (i, 0))
    residual = pl.pallas_call(
        functools.partial(final_kernel, nch, chunk),
        grid=(rows // ft,),
        out_shape=jax.ShapeDtypeStruct((rows, cols), bf16),
        in_specs=[
            vmem, block(cols), block(rank), block(rank), block(rank), vmem, vmem,
        ],
        out_specs=block(cols),
        compiler_params=pltpu.CompilerParams(vmem_limit_bytes=50_000_000),
        name="residual",
    )(steps, matrix, left, left_round, left_new, right, right_t)
    descent = right_t.transpose(0, 2, 1).reshape(cols, rank).astype(f32)
    right_new = (right.astype(f32) + steps[1, 0] * descent).astype(bf16)
    return (left_new, right_new, residual)


def solution(mesh):
    placed = (
        P(("grp", "col"), "row"),
        P(("grp", "row"), "col"),
        P(("grp", "row"), "col"),
        P(("grp", "row"), None),
        P(("grp", "col"), None),
    )
    return jax.shard_map(
        functools.partial(body, mesh.shape["row"], mesh.shape["col"]),
        mesh=mesh,
        in_specs=placed,
        out_specs=(P(("grp", "row"), None), P(("grp", "col"), None), P(("grp", "row"), "col")),
        check_vma=False,
    )
```

time: 490 us -> 247 us (0.50)
  waiting for transfers between devices: 229 us -> 0 us
  Pallas kernels: 0 us -> 228 us
  matrix products: 135 us -> 0 us
  blocking collectives: 64.8 us -> 0 us
  other arithmetic: 42.5 us -> 9.56 us
  between operations: 17.7 us -> 0.67 us
  local copies, waits for them, and re-layouts: 0.01 us -> 8.3 us
    pallas_call x0 -> x2, Pallas kernels: none -> 228 us  [the longest x1 211 us: body(): pl.pallas_call(functools.partial(main_kernel, nr, nc, nch, chunk, tile),...]
    dot_general x6 -> x0, matrix products: 135 us -> none  [the longest x3 67.3 us: contract_rank(): lax.dot_general(first, second, (((1,), (1,)), ((), ())), preferred_elemen...]
    psum x2 -> x0, waiting for transfers between devices: 133 us -> none  [the longest x1 92 us: body(): lax.psum(right_partial.astype(jnp.bfloat16), 'row').astype(jnp.float32)]
    all_gather x2 -> x0, waiting for transfers between devices: 94.6 us -> none  [the longest x1 91 us: body(): grads_full = lax.all_gather(out_grads, 'row', axis=0, tiled=True)]
    psum x2 -> x0, blocking collectives: 64.8 us -> none  [the longest x1 32.8 us: body(): lax.psum((jnp.sum(fisher * left_image * left_image), left_norm_term), ('r...]
    convert_element_type x3 -> x1, other arithmetic: 36.6 us -> 4.42 us  [body(): right_new = (right.astype(f32) + steps[1, 0] * descent).astype(bf16)]
    mul x0 -> x1, local copies, waits for them, and re-layouts: none -> 6.21 us  [body(): right_new = (right.astype(f32) + steps[1, 0] * descent).astype(bf16)]
    reduce_sum x2 -> x0, other arithmetic: 5.9 us -> none  [the longest x1 3.48 us: body(): right_norm_term = jnp.sum(right_descent * right_descent) / row_count]
  transfers between devices with their start and end apart: 4 -> 0, of which waited for: 4 -> 0; matrix products, arithmetic and copies ran while one was open for 4% -> 0% of each run, Pallas kernels for 0% -> 0%
where the time goes in v1:
time: 247 us
  Pallas kernels  228 us (92%)
  other arithmetic  9.56 us (4%)
  local copies, waits for them, and re-layouts  8.3 us (3%)
    pallas_call x1, Pallas kernels, body(): pl.pallas_call(functools.partial(main_kernel, nr, nc, nch, chunk, tile),...  211 us
    pallas_call x1, Pallas kernels, body(): pl.pallas_call(functools.partial(final_kernel, nch, chunk), grid=(rows //...  17.5 us
    mul x1, local copies, waits for them, and re-layouts, body(): right_new = (right.astype(f32) + steps[1, 0] * descent).astype(bf16)  6.21 us
    mul x1, other arithmetic, body(): right_new = (right.astype(f32) + steps[1, 0] * descent).astype(bf16)  5.14 us

profile of v1, /device:TPU:0, one launch (start us, length us, event | category | flops | bytes accessed | tf_op | source)
XLA Modules:
  0.0 246.7 jit_solution(11301779873817331130)
XLA Ops:
  0.6 210.6 %factor_steps.1 = (bf16[1536,256]{1,0:T(8,128)(2,1)}, bf16[1536,256]{1,0:T(8,128)(2,1)}, bf16[9,256,512]{2,1,0:T(8,128)(2,1)}, f32[2,128]{1,0:T(2,128)}) custom-call(bf16[128,1536]{1,0:T(8,128)(2,1)} %act_hbm.1, bf16[128,4608]{1,0:T(8,128)(2,1)} %og_hbm.1, bf16[1536,4608]{1,0:T(8,128)(2,1)} %w_ref.1, bf16[1536,256]{1,0:T(8,128)(2,1)} %l_ref.3, ...), custom_call_target="tpu_custom_call" | custom-call | tf_op jit(solution)/shard_map/factor_steps/pallas_call | solution.py:466
  211.3 1.2 slice.3
  212.5 5.1 %multiply_bitcast_fusion = f32[9,512,256]{1,2,0:T(8,128)} fusion(bf16[9,256,512]{2,1,0:T(8,128)(2,1)} %get-tuple-element.9.t_ref, f32[]{:T(128)} %bitcast), kind=kLoop, calls=%fused_computation.2 | loop fusion | flops 2359296 | bytes 7077892 | tf_op jit(solution)/shard_map/mul | solution.py:522
  217.6 0.0 copy-start
  217.6 6.2 %copy.8 = f32[9,512,256]{2,1,0:T(8,128)} copy(f32[9,512,256]{1,2,0:T(8,128)} %multiply_bitcast_fusion) | data formatting | bytes 9437184 | tf_op jit(solution)/shard_map/mul | solution.py:522
  223.8 0.0 copy-done
  223.8 0.0 copy-start.1
  223.8 0.0 copy-start.2
  223.8 0.0 copy-start.3
  223.8 0.0 copy-start.4
  223.8 4.4 %fusion = bf16[4608,256]{1,0:T(8,128)(2,1)} fusion(f32[9,512,256]{2,1,0:T(8,128)} %copy.8, bf16[4608,256]{1,0:T(8,128)(2,1)S(1)} %copy-done), kind=kLoop, calls=%fused_computation.1 | loop fusion | flops 3538944 | bytes 9437184 | tf_op jit(solution)/shard_map/convert_element_type | solution.py:522
  228.3 0.0 copy-done.1
  228.3 0.0 copy-done.2
  228.3 0.0 copy-done.3
  228.3 0.0 copy-done.4
  228.3 17.5 %residual.1 = bf16[1536,4608]{1,0:T(8,128)(2,1)} custom-call(f32[2,128]{1,0:T(2,128)S(1)} %copy-done.4, bf16[1536,4608]{1,0:T(8,128)(2,1)} %w_ref.1, bf16[1536,256]{1,0:T(8,128)(2,1)S(1)} %copy-done.1, bf16[1536,256]{1,0:T(8,128)(2,1)S(1)} %copy-done.3, bf16[1536,256]{1,0:T(8,128)(2,1)S(1)} %copy-done.2, bf16[4608,256]{1,0:T(8,128)(2,1)S(1)} %copy-done, ...), custom_call_target="tpu_custom_call" | custom-call | tf_op jit(solution)/shard_map/residual/pallas_call | solution.py:510
  245.8 0.9 copy.10
Async XLA Ops:
  217.6 6.2 %copy-start = (bf16[4608,256]{1,0:T(8,128)(2,1)S(1)}, bf16[4608,256]{1,0:T(8,128)(2,1)}, u32[]{:S(2)}) copy-start(bf16[4608,256]{1,0:T(8,128)(2,1)} %r_ref.3) | copy-start | bytes 7077892
  223.8 4.4 %copy-start.1 = (bf16[1536,256]{1,0:T(8,128)(2,1)S(1)}, bf16[1536,256]{1,0:T(8,128)(2,1)}, u32[]{:S(2)}) copy-start(bf16[1536,256]{1,0:T(8,128)(2,1)} %l_ref.3) | copy-start | bytes 2359300
  223.8 4.4 %copy-start.2 = (bf16[1536,256]{1,0:T(8,128)(2,1)S(1)}, bf16[1536,256]{1,0:T(8,128)(2,1)}, u32[]{:S(2)}) copy-start(bf16[1536,256]{1,0:T(8,128)(2,1)} %get-tuple-element.14.ln_ref) | copy-start | bytes 2359300
  223.8 4.4 %copy-start.3 = (bf16[1536,256]{1,0:T(8,128)(2,1)S(1)}, bf16[1536,256]{1,0:T(8,128)(2,1)}, u32[]{:S(2)}) copy-start(bf16[1536,256]{1,0:T(8,128)(2,1)} %get-tuple-element.10.ldr_ref) | copy-start | bytes 2359300
  223.8 4.4 %copy-start.4 = (f32[2,128]{1,0:T(2,128)S(1)}, f32[2,128]{1,0:T(2,128)}, u32[]{:S(2)}) copy-start(f32[2,128]{1,0:T(2,128)} %get-tuple-element.8.s_ref) | copy-start | bytes 3076

commit v2 on v1

--- a/solution.py
+++ b/solution.py
@@ -8,6 +8,9 @@
 from jax.sharding import PartitionSpec as P
 
 epsilon = 1e-06
+CHUNK = 256
+TILE = 512
+SPAN = 3
 f32 = jnp.float32
 bf16 = jnp.bfloat16
 MESH = pl.DeviceIdType.MESH
@@ -25,19 +28,15 @@
     return jnp.dot(a, b, preferred_element_type=f32)
 
 
-def mm_nt(a, b):
-    return lax.dot_general(a, b, (((1,), (1,)), ((), ())), preferred_element_type=f32)
-
-
 def main_kernel(
     nr, nc, nch, chunk, tile,
     act_hbm, og_hbm, w_hbm, l_ref, r_ref,
-    ln_ref, ldr_ref, t_hbm, s_ref,
-    fisher, wbuf, ogb, actb, actt, lpart, lsend, lr1, lh, lr2, ld4, lnt,
-    part, inb, exb, tot, rp, acc, sc, sr,
+    ln_ref, ldr_ref, t_hbm, rt_hbm, s_ref,
+    fisher, wbuf, ogb, actb, actt, rt, lpart, lsend, lr1, lh, lr2, ld4, lnt,
+    part, inb, exb, tot, acc, sc, sr,
     wsem, ogsem, asem, act_s, act_r, up_s, up_r, dn_s, dn_r,
     l1, l2s, l2r, l3s, l3r, l4, cs, cr, rs, rr,
-    in_s, in_r, ex_s, ex_r, out_s, out_r, tsem,
+    in_s, in_r, ex_s, ex_r, out_s, out_r, tsem, rtsem,
 ):
     g = lax.axis_index("grp")
     r = lax.axis_index("row")
@@ -115,7 +114,7 @@
     acc[...] = jnp.zeros_like(acc)
 
     def rows_at(i):
-        return pl.ds(pl.multiple_of(i * tile, tile), tile)
+        return pl.ds(i * tile, tile)
 
     def cols_at(k):
         return pl.ds(pl.multiple_of(k * chunk, chunk), chunk)
@@ -125,20 +124,22 @@
         w_copy(lax.rem(k + 1, nch), lax.rem(k + 1, 2)).start()
         w_copy(k, slot).wait()
 
-        def step(i, carry):
+        og = ogb[k].reshape(-1, chunk)
+        rj = r_ref[cols_at(k), :]
+        for i in range(nt):
             rw = rows_at(i)
-            og = ogb[k].reshape(-1, chunk)
             grad = mm(actt[rw, :], og)
             w = wbuf[slot, rw, :].astype(f32)
-            rj = r_ref[cols_at(k), :]
             wg = w * grad
             fish = 1.0 + wg * wg
             fisher[k, rw, :] = fish
-            early = w - mm_nt(l_ref[rw, :], rj)
+            early = w - mm(l_ref[rw, :], rt[k])
             lpart[rw, :] += mm((fish * early).astype(bf16), rj)
-            return carry
-
-        lax.fori_loop(0, nt, step, 0)
+
+    def turn_right(k, carry):
+        rt[k] = r_ref[cols_at(k), :].astype(f32).T.astype(bf16)
+        pltpu.make_async_copy(rt.at[k], rt_hbm.at[k], rtsem.at[k]).start()
+        return carry
 
     def gather_step(j, carry):
         @pl.when(j < nch)
@@ -187,6 +188,7 @@
                 return carry
 
             lax.fori_loop(0, rows // lanes, turn, 0)
+            lax.fori_loop(0, nch, turn_right, 0)
 
         @pl.when(j >= nr - 1)
         def _():
@@ -242,30 +244,28 @@
     for k in range(nc):
         lpart[k * q:(k + 1) * q, :] = ld4[k % 2, k // 2].astype(f32)
 
-    def cast_left(i, carry):
+    for i in range(nt):
         ldr_ref[rows_at(i), :] = lpart[rows_at(i), :].astype(bf16)
-        return carry
-
-    lax.fori_loop(0, nt, cast_left, 0)
-
-    def curve_tile(fish, image):
-        weighted = fish * image * image
-        acc[...] += jnp.sum(weighted.reshape(tile // 8, 8, chunk), axis=0)
+
+    def curve(k, lhs_ref, rhs):
+        found = acc[...]
+        for i in range(nt):
+            rw = rows_at(i)
+            image = mm(lhs_ref[rw, :], rhs)
+            weighted = fisher[k, rw, :] * image * image
+            found = found + jnp.sum(weighted.reshape(tile // 8, 8, chunk), axis=0)
+        acc[...] = found
 
     def pass_b(k, carry):
-        def step(i, inner):
-            rw = rows_at(i)
-            curve_tile(fisher[k, rw, :], mm_nt(ldr_ref[rw, :], r_ref[cols_at(k), :]))
-            return inner
-
-        return lax.fori_loop(0, nt, step, carry)
+        curve(k, ldr_ref, rt[k])
+        return carry
 
     lax.fori_loop(0, nch, pass_b, 0)
 
     def total(t, norm_part):
-        curve = jnp.sum(jnp.sum(acc[...], axis=0, keepdims=True), axis=1, keepdims=True)
+        bend = jnp.sum(jnp.sum(acc[...], axis=0, keepdims=True), axis=1, keepdims=True)
         top = lax.broadcasted_iota(jnp.int32, (8, 128), 0) == 0
-        sc[t, c] = jnp.where(top, jnp.broadcast_to(curve, (8, 128)), jnp.broadcast_to(norm_part, (8, 128)))
+        sc[t, c] = jnp.where(top, jnp.broadcast_to(bend, (8, 128)), jnp.broadcast_to(norm_part, (8, 128)))
         for d in range(1, nc):
             remote(sc.at[t, c], sc.at[t, c], cs.at[t, d - 1], cr.at[t, d - 1], at(r, lax.rem(c + d, nc))).start()
         for d in range(1, nc):
@@ -282,14 +282,11 @@
 
     s_ref[0:1, :] = total(0, norm)
 
-    def make_left(i, carry):
+    for i in range(nt):
         rw = rows_at(i)
         new = (l_ref[rw, :].astype(f32) + s_ref[0:1, 0:1] * lpart[rw, :]).astype(bf16)
         ln_ref[rw, :] = new
         lnt[i] = new.astype(f32).T.astype(bf16)
-        return carry
-
-    lax.fori_loop(0, nt, make_left, 0)
     acc[...] = jnp.zeros_like(acc)
 
     half = nr // 2
@@ -318,26 +315,16 @@
             w_copy(k + 1, lax.rem(k + 1 + nch, 2)).start()
 
         w_copy(k, slot).wait()
-        rp[...] = jnp.zeros_like(rp)
-
-        def step(i, carry):
+        moved = jnp.zeros((l_ref.shape[1], chunk), f32)
+        for i in range(nt):
             rw = rows_at(i)
-            rj = r_ref[cols_at(k), :]
-            later = wbuf[slot, rw, :].astype(f32) - mm_nt(l_ref[rw, :], rj)
-            later = later - s_ref[0:1, 0:1] * mm_nt(ldr_ref[rw, :], rj)
-            rp[...] += mm(lnt[i], (fisher[k, rw, :] * later).astype(bf16))
-            return carry
-
-        lax.fori_loop(0, nt, step, 0)
-        part[k] = rp[...].astype(bf16)
+            later = wbuf[slot, rw, :].astype(f32) - mm(l_ref[rw, :], rt[k])
+            later = later - s_ref[0:1, 0:1] * mm(ldr_ref[rw, :], rt[k])
+            moved = moved + mm(lnt[i], (fisher[k, rw, :] * later).astype(bf16))
+        part[k] = moved.astype(bf16)
 
     def pass_d(k):
-        def step(i, carry):
-            rw = rows_at(i)
-            curve_tile(fisher[k, rw, :], mm(ln_ref[rw, :], tot[k]))
-            return carry
-
-        lax.fori_loop(0, nt, step, 0)
+        curve(k, ln_ref, tot[k])
 
     lag = 2
 
@@ -420,6 +407,7 @@
 
     def drain_right(k, carry):
         pltpu.make_async_copy(tot.at[k], t_hbm.at[k], tsem.at[k]).wait()
+        pltpu.make_async_copy(rt.at[k], rt_hbm.at[k], rtsem.at[k]).wait()
 
         @pl.when(not_mid)
         def _():
@@ -437,14 +425,17 @@
     lax.fori_loop(0, nch, drain_right, 0)
 
 
-def final_kernel(nch, chunk, s_ref, w_ref, l_ref, ldr_ref, ln_ref, r_ref, t_ref, o_ref):
+def final_kernel(span, chunk, tile, s_ref, w_ref, l_ref, ldr_ref, ln_ref, r_ref, rt_ref, t_ref, o_ref, rn_ref):
     s1 = s_ref[0:1, 0:1]
     s2 = s_ref[1:2, 0:1]
-    for k in range(nch):
+    for k in range(span):
         cols = slice(k * chunk, (k + 1) * chunk)
-        rj = r_ref[cols, :]
-        out = w_ref[:, cols].astype(f32) - mm_nt(l_ref[...], rj) - s1 * mm_nt(ldr_ref[...], rj)
-        o_ref[:, cols] = (out - s2 * mm(ln_ref[...], t_ref[k])).astype(bf16)
+        rn_ref[cols, :] = (r_ref[cols, :].astype(f32) + s2 * t_ref[k].astype(f32).T).astype(bf16)
+
+        for i in range(l_ref.shape[0] // tile):
+            rw = slice(i * tile, (i + 1) * tile)
+            out = w_ref[rw, cols].astype(f32) - mm(l_ref[rw, :], rt_ref[k]) - s1 * mm(ldr_ref[rw, :], rt_ref[k])
+            o_ref[rw, cols] = (out - s2 * mm(ln_ref[rw, :], t_ref[k])).astype(bf16)
 
 
 def body(nr, nc, activations, out_grads, matrix, left, right):
@@ -452,9 +443,9 @@
     rank = left.shape[1]
     ctok = activations.shape[0]
     rtok = out_grads.shape[0]
-    chunk = pick(cols, 512, 128)
+    chunk = pick(cols, CHUNK, 128)
     nch = cols // chunk
-    tile = pick(rows, 256, 16)
+    tile = pick(rows, TILE, 16)
     nx = nc // 2
     q = rows // nc
     dma = pltpu.SemaphoreType.DMA
@@ -463,22 +454,24 @@
     px = max(nx - 1, 1)
     pr = max(nr - 1, 1)
     pc = max(nc - 1, 1)
-    left_new, left_round, right_t, steps = pl.pallas_call(
+    left_new, left_round, descent_t, right_t, steps = pl.pallas_call(
         functools.partial(main_kernel, nr, nc, nch, chunk, tile),
         out_shape=(
             jax.ShapeDtypeStruct((rows, rank), bf16),
             jax.ShapeDtypeStruct((rows, rank), bf16),
             jax.ShapeDtypeStruct((nch, rank, chunk), bf16),
+            jax.ShapeDtypeStruct((nch, rank, chunk), bf16),
             jax.ShapeDtypeStruct((2, 128), f32),
         ),
         in_specs=[any_spec, any_spec, any_spec, vmem, vmem],
-        out_specs=(vmem, vmem, any_spec, vmem),
+        out_specs=(vmem, vmem, any_spec, any_spec, vmem),
         scratch_shapes=[
             pltpu.VMEM((nch, rows, chunk), f32),
             pltpu.VMEM((2, rows, chunk), bf16),
             pltpu.VMEM((nch, nr, rtok, chunk), bf16),
             pltpu.VMEM((nc, ctok, rows), bf16),
             pltpu.VMEM((rows, nc * ctok), bf16),
+            pltpu.VMEM((nch, rank, chunk), bf16),
             pltpu.VMEM((rows, rank), f32),
             pltpu.VMEM((2, nx, q, rank), bf16),
             pltpu.VMEM((nx, q, rank), bf16),
@@ -490,7 +483,6 @@
             pltpu.VMEM((nch, rank, chunk), bf16),
             pltpu.VMEM((nch, rank, chunk), bf16),
             pltpu.VMEM((nch, rank, chunk), bf16),
-            pltpu.VMEM((rank, chunk), f32),
             pltpu.VMEM((8, chunk), f32),
             pltpu.VMEM((2, nc, 8, 128), f32),
             pltpu.VMEM((2, nr, 8, 128), f32),
@@ -498,28 +490,29 @@
             dma((nch, pr)), dma((nch, pr)), dma((nch, pr)), dma((nch, pr)),
             dma((2,)), dma((px,)), dma((px,)), dma((px,)), dma((px,)), dma((2,)),
             dma((2, pc)), dma((2, pc)), dma((2, pr)), dma((2, pr)),
-            dma((nch,)), dma((nch,)), dma((nch,)), dma((nch,)), dma((nch,)), dma((nch,)), dma((nch,)),
+            dma((nch,)), dma((nch,)), dma((nch,)), dma((nch,)), dma((nch,)), dma((nch,)), dma((nch,)), dma((nch,)),
         ],
         compiler_params=pltpu.CompilerParams(
             collective_id=0, has_side_effects=True, vmem_limit_bytes=66_500_000
         ),
         name="factor_steps",
     )(activations, out_grads, matrix, left, right)
-    ft = pick(rows, 256, 16)
-    block = lambda width: pl.BlockSpec((ft, width), lambda i: (i, 0))
-    residual = pl.pallas_call(
-        functools.partial(final_kernel, nch, chunk),
-        grid=(rows // ft,),
-        out_shape=jax.ShapeDtypeStruct((rows, cols), bf16),
-        in_specs=[
-            vmem, block(cols), block(rank), block(rank), block(rank), vmem, vmem,
-        ],
-        out_specs=block(cols),
+    span = pick(nch, SPAN, 1)
+    wide = pl.BlockSpec((rows, span * chunk), lambda i: (0, i))
+    tall = pl.BlockSpec((span * chunk, rank), lambda i: (i, 0))
+    turned = pl.BlockSpec((span, rank, chunk), lambda i: (i, 0, 0))
+    residual, right_new = pl.pallas_call(
+        functools.partial(final_kernel, span, chunk, tile),
+        grid=(nch // span,),
+        out_shape=(
+            jax.ShapeDtypeStruct((rows, cols), bf16),
+            jax.ShapeDtypeStruct((cols, rank), bf16),
+        ),
+        in_specs=[vmem, wide, vmem, vmem, vmem, tall, turned, turned],
+        out_specs=(wide, tall),
         compiler_params=pltpu.CompilerParams(vmem_limit_bytes=50_000_000),
         name="residual",
-    )(steps, matrix, left, left_round, left_new, right, right_t)
-    descent = right_t.transpose(0, 2, 1).reshape(cols, rank).astype(f32)
-    right_new = (right.astype(f32) + steps[1, 0] * descent).astype(bf16)
+    )(steps, matrix, left, left_round, left_new, right, right_t, descent_t)
     return (left_new, right_new, residual)
 
 

time: 247 us -> 220 us (0.89)
  Pallas kernels: 228 us -> 212 us
  other arithmetic: 9.56 us -> 0 us
    pallas_call x1, Pallas kernels: 211 us -> 194 us  [body(): pl.pallas_call(functools.partial(main_kernel, nr, nc, nch, chunk, tile),...]
    mul x1 -> x0, local copies, waits for them, and re-layouts: 6.21 us -> none  [body(): right_new = (right.astype(f32) + steps[1, 0] * descent).astype(bf16)]
    unnamed x11, local copies, waits for them, and re-layouts: 0.9 us -> 6.57 us
    mul x1 -> x0, other arithmetic: 5.14 us -> none  [body(): right_new = (right.astype(f32) + steps[1, 0] * descent).astype(bf16)]
    convert_element_type x1 -> x0, other arithmetic: 4.42 us -> none  [body(): right_new = (right.astype(f32) + steps[1, 0] * descent).astype(bf16)]
where the time goes in v2:
time: 220 us; the launch traced here: 219 us
  Pallas kernels  212 us (96%)
  local copies, waits for them, and re-layouts  6.57 us (3%)
    pallas_call x1, Pallas kernels, body(): pl.pallas_call(functools.partial(main_kernel, nr, nc, nch, chunk, tile),...  194 us
    pallas_call x1, Pallas kernels, body(): pl.pallas_call(functools.partial(final_kernel, span, chunk, tile), grid=(...  18 us
    unnamed x11, local copies, waits for them, and re-layouts  6.57 us

profile of v2, /device:TPU:0, one launch (start us, length us, event | category | flops | bytes accessed | tf_op | source)
XLA Modules:
  0.0 219.4 jit_solution(1655719303796956664)
XLA Ops:
  0.6 194.2 %factor_steps.1 = (bf16[1536,256]{1,0:T(8,128)(2,1)}, bf16[1536,256]{1,0:T(8,128)(2,1)}, bf16[18,256,256]{2,1,0:T(8,128)(2,1)}, bf16[18,256,256]{2,1,0:T(8,128)(2,1)}, f32[2,128]{1,0:T(2,128)}) custom-call(bf16[128,1536]{1,0:T(8,128)(2,1)} %act_hbm.1, bf16[128,4608]{1,0:T(8,128)(2,1)} %og_hbm.1, bf16[1536,4608]{1,0:T(8,128)(2,1)} %w_ref.1, ...), custom_call_target="tpu_custom_call" | custom-call | tf_op jit(solution)/shard_map/factor_steps/pallas_call | solution.py:457
  194.9 0.0 copy-start
  194.9 1.7 copy-done
  196.5 0.0 copy-start.1
  196.5 1.1 copy-done.1
  197.7 0.0 copy-start.2
  197.7 1.1 copy-done.2
  198.8 0.0 copy-start.3
  198.8 1.1 copy-done.3
  199.9 0.0 copy-start.4
  200.0 0.6 copy-done.4
  200.6 18.0 %residual.1 = (bf16[1536,4608]{1,0:T(8,128)(2,1)}, bf16[4608,256]{1,0:T(8,128)(2,1)}) custom-call(f32[2,128]{1,0:T(2,128)S(1)} %copy-done.4, bf16[1536,4608]{1,0:T(8,128)(2,1)} %w_ref.1, bf16[1536,256]{1,0:T(8,128)(2,1)S(1)} %copy-done.1, bf16[1536,256]{1,0:T(8,128)(2,1)S(1)} %copy-done.3, bf16[1536,256]{1,0:T(8,128)(2,1)S(1)} %copy-done.2, ...), custom_call_target="tpu_custom_call" | custom-call | tf_op jit(solution)/shard_map/residual/pallas_call | solution.py:504
  218.6 0.9 copy.9
Async XLA Ops:
  194.9 1.7 copy-start
  196.5 1.1 copy-start.1
  197.7 1.1 copy-start.2
  198.8 1.1 copy-start.3
  199.9 0.6 copy-start.4

commit v3 on v2

--- a/solution.py
+++ b/solution.py
@@ -30,13 +30,14 @@
 
 def main_kernel(
     nr, nc, nch, chunk, tile,
-    act_hbm, og_hbm, w_hbm, l_ref, r_ref,
-    ln_ref, ldr_ref, t_hbm, rt_hbm, s_ref,
+    act_hbm, og_hbm, w_hbm, l_hbm, r_hbm,
+    ln_hbm, ldr_hbm, t_hbm, rt_hbm, s_ref,
+    l_ref, r_ref, ln_ref, ldr_ref,
     fisher, wbuf, ogb, actb, actt, rt, lpart, lsend, lr1, lh, lr2, ld4, lnt,
     part, inb, exb, tot, acc, sc, sr,
     wsem, ogsem, asem, act_s, act_r, up_s, up_r, dn_s, dn_r,
     l1, l2s, l2r, l3s, l3r, l4, cs, cr, rs, rr,
-    in_s, in_r, ex_s, ex_r, out_s, out_r, tsem, rtsem,
+    in_s, in_r, ex_s, ex_r, out_s, out_r, tsem, rtsem, iosem,
 ):
     g = lax.axis_index("grp")
     r = lax.axis_index("row")
@@ -72,6 +73,12 @@
 
     lax.fori_loop(0, nch, start_og, 0)
     w_copy(0, 0).start()
+    l_in = pltpu.make_async_copy(l_hbm, l_ref, iosem.at[0])
+    r_in = pltpu.make_async_copy(r_hbm, r_ref, iosem.at[1])
+    ldr_out = pltpu.make_async_copy(ldr_ref, ldr_hbm, iosem.at[2])
+    ln_out = pltpu.make_async_copy(ln_ref, ln_hbm, iosem.at[3])
+    l_in.start()
+    r_in.start()
 
     bar = pltpu.get_barrier_semaphore()
     for d in range(1, nr):
@@ -111,6 +118,8 @@
         remote(ogb.at[k, blk], ogb.at[k, blk], dn_s.at[k, s], dn_r.at[k, s], at(jnp.maximum(r - 1, 0), c)).wait_recv()
 
     lpart[...] = jnp.zeros_like(lpart)
+    l_in.wait()
+    r_in.wait()
     acc[...] = jnp.zeros_like(acc)
 
     def rows_at(i):
@@ -246,6 +255,7 @@
 
     for i in range(nt):
         ldr_ref[rows_at(i), :] = lpart[rows_at(i), :].astype(bf16)
+    ldr_out.start()
 
     def curve(k, lhs_ref, rhs):
         found = acc[...]
@@ -287,6 +297,7 @@
         new = (l_ref[rw, :].astype(f32) + s_ref[0:1, 0:1] * lpart[rw, :]).astype(bf16)
         ln_ref[rw, :] = new
         lnt[i] = new.astype(f32).T.astype(bf16)
+    ln_out.start()
     acc[...] = jnp.zeros_like(acc)
 
     half = nr // 2
@@ -423,6 +434,8 @@
         return carry
 
     lax.fori_loop(0, nch, drain_right, 0)
+    ldr_out.wait()
+    ln_out.wait()
 
 
 def final_kernel(span, chunk, tile, s_ref, w_ref, l_ref, ldr_ref, ln_ref, r_ref, rt_ref, t_ref, o_ref, rn_ref):
@@ -463,9 +476,13 @@
             jax.ShapeDtypeStruct((nch, rank, chunk), bf16),
             jax.ShapeDtypeStruct((2, 128), f32),
         ),
-        in_specs=[any_spec, any_spec, any_spec, vmem, vmem],
-        out_specs=(vmem, vmem, any_spec, any_spec, vmem),
+        in_specs=[any_spec] * 5,
+        out_specs=(any_spec, any_spec, any_spec, any_spec, vmem),
         scratch_shapes=[
+            pltpu.VMEM((rows, rank), bf16),
+            pltpu.VMEM((cols, rank), bf16),
+            pltpu.VMEM((rows, rank), bf16),
+            pltpu.VMEM((rows, rank), bf16),
             pltpu.VMEM((nch, rows, chunk), f32),
             pltpu.VMEM((2, rows, chunk), bf16),
             pltpu.VMEM((nch, nr, rtok, chunk), bf16),
@@ -490,7 +507,7 @@
             dma((nch, pr)), dma((nch, pr)), dma((nch, pr)), dma((nch, pr)),
             dma((2,)), dma((px,)), dma((px,)), dma((px,)), dma((px,)), dma((2,)),
             dma((2, pc)), dma((2, pc)), dma((2, pr)), dma((2, pr)),
-            dma((nch,)), dma((nch,)), dma((nch,)), dma((nch,)), dma((nch,)), dma((nch,)), dma((nch,)), dma((nch,)),
+            dma((nch,)), dma((nch,)), dma((nch,)), dma((nch,)), dma((nch,)), dma((nch,)), dma((nch,)), dma((nch,)), dma((4,)),
         ],
         compiler_params=pltpu.CompilerParams(
             collective_id=0, has_side_effects=True, vmem_limit_bytes=66_500_000
@@ -500,6 +517,7 @@
     span = pick(nch, SPAN, 1)
     wide = pl.BlockSpec((rows, span * chunk), lambda i: (0, i))
     tall = pl.BlockSpec((span * chunk, rank), lambda i: (i, 0))
+    flat = pl.BlockSpec((rows, rank), lambda i: (0, 0))
     turned = pl.BlockSpec((span, rank, chunk), lambda i: (i, 0, 0))
     residual, right_new = pl.pallas_call(
         functools.partial(final_kernel, span, chunk, tile),
@@ -508,9 +526,9 @@
             jax.ShapeDtypeStruct((rows, cols), bf16),
             jax.ShapeDtypeStruct((cols, rank), bf16),
         ),
-        in_specs=[vmem, wide, vmem, vmem, vmem, tall, turned, turned],
+        in_specs=[vmem, wide, flat, flat, flat, tall, turned, turned],
         out_specs=(wide, tall),
-        compiler_params=pltpu.CompilerParams(vmem_limit_bytes=50_000_000),
+        compiler_params=pltpu.CompilerParams(vmem_limit_bytes=66_500_000),
         name="residual",
     )(steps, matrix, left, left_round, left_new, right, right_t, descent_t)
     return (left_new, right_new, residual)

time: 220 us -> 214 us (0.973)
  local copies, waits for them, and re-layouts: 6.57 us -> 2.06 us
    unnamed x11 -> x1, local copies, waits for them, and re-layouts: 6.57 us -> 2.06 us
    pallas_call x1, Pallas kernels: 194 us -> 192 us  [body(): pl.pallas_call(functools.partial(main_kernel, nr, nc, nch, chunk, tile),...]
where the time goes in v3:
time: 214 us
  Pallas kernels  211 us (99%)
    pallas_call x1, Pallas kernels, body(): pl.pallas_call(functools.partial(main_kernel, nr, nc, nch, chunk, tile),...  192 us
    pallas_call x1, Pallas kernels, body(): pl.pallas_call(functools.partial(final_kernel, span, chunk, tile), grid=(...  19.2 us

profile of v3, /device:TPU:0, one launch (start us, length us, event | category | flops | bytes accessed | tf_op | source)
XLA Modules:
  0.0 213.8 jit_solution(13943770102976873027)
XLA Ops:
  0.6 191.9 %factor_steps.1 = (bf16[1536,256]{1,0:T(8,128)(2,1)}, bf16[1536,256]{1,0:T(8,128)(2,1)}, bf16[18,256,256]{2,1,0:T(8,128)(2,1)}, bf16[18,256,256]{2,1,0:T(8,128)(2,1)}, f32[2,128]{1,0:T(2,128)}) custom-call(bf16[128,1536]{1,0:T(8,128)(2,1)} %act_hbm.1, bf16[128,4608]{1,0:T(8,128)(2,1)} %og_hbm.1, bf16[1536,4608]{1,0:T(8,128)(2,1)} %w_ref.1, ...), custom_call_target="tpu_custom_call" | custom-call | tf_op jit(solution)/shard_map/factor_steps/pallas_call | solution.py:470
  192.6 19.2 %residual.1 = (bf16[1536,4608]{1,0:T(8,128)(2,1)}, bf16[4608,256]{1,0:T(8,128)(2,1)}) custom-call(f32[2,128]{1,0:T(2,128)} %get-tuple-element.11.s_ref, bf16[1536,4608]{1,0:T(8,128)(2,1)} %w_ref.1, bf16[1536,256]{1,0:T(8,128)(2,1)} %l_ref.1, bf16[1536,256]{1,0:T(8,128)(2,1)} %get-tuple-element.12.ldr_ref, bf16[1536,256]{1,0:T(8,128)(2,1)} %get-tuple-element.20.ln_ref, ...), custom_call_target="tpu_custom_call" | custom-call | tf_op jit(solution)/shard_map/residual/pallas_call | solution.py:522
  211.7 2.1 copy.9
